TPU v7x, 128 devices: a whole 4x4x4 slice. The times are simulated.
128 devices in a mesh: blk: 16 (over y, x_hi, core), rep: 8 (over x_lo, z).
Axes of the slice: x: 4 (x_hi: 2, x_lo: 2; x = x_hi * 2 + x_lo), y: 4, z: 4, core: 2. Of those that a mesh axis runs over, the one named last changes fastest.
Arguments:
- cotangent: bfloat16 [512, 256, 128], P('blk', 'rep'), may hold values from -6 to 6
- relu_mask: int32 [512, 256, 128], P('blk', 'rep'), may hold values 0 or 1
- aggregated: bfloat16 [512, 256, 128], P('blk', 'rep'), may hold values from -6 to 6
- weight: bfloat16 [256, 256], P('rep'), may hold values from -0.375 to 0.375
- tiles: bfloat16 [512, 16, 128, 128], P('blk'), may hold values from -0.125 to 0.125
- col_block: int32 [512, 16], P('blk'), may hold values from 0 to 511, as said below
- live_count: int32 [512], P('blk'), may hold values from 1 to 16, as said below
Outputs:
- input_grad: bfloat16 [512, 256, 128], P('blk', 'rep')
- weight_grad: float32 [256, 256], P('rep')
Inputs may be any that keep to these rules, and one draw needn't show every extreme that they name: The slab of a row block b is b // 32; the slab of col_block[b, s] lies at most 2 slabs from it around the closed cycle of the 16 slabs, and both distance 2 directions occur. `live_count`: row blocks of one slab share a density level, so live counts differ from slab to slab; some row block has all 16 slots live.
All inputs are finite; a program needn't handle non-finite values. No bound on the sum of `relu_mask` on one device may be relied on, other than what follows from the above.
Results may differ from a plain program's by a relative error of at most 0.0049.
Values may be sent and summed in bfloat16 or wider, within the bound.
A program may use at most 128 MiB of HBM per device.

v0:
```python
import math
import jax
import jax.numpy as jnp
from jax import lax
from jax.sharding import PartitionSpec as P

REACH = 2


def from_behind(value, axis, steps):
    count = lax.axis_size(axis)
    pairs = [(source, (source + steps) % count) for source in range(count)]
    return lax.ppermute(value, axis, pairs)


def on_device(cotangent, relu_mask, aggregated, weight, tiles, col_block, live_count):
    blocks_here = cotangent.shape[0]
    cols_here = cotangent.shape[1]
    tile_size = cotangent.shape[2]
    grad_z = cotangent * relu_mask.astype(jnp.bfloat16)
    gathered_part = lax.all_gather(grad_z, "rep", axis=1, tiled=True)
    grad_h = jnp.einsum("io,bon->bin", weight, gathered_part, preferred_element_type=jnp.float32)
    col_part = jnp.einsum(
        "bin,bon->io", aggregated, gathered_part, preferred_element_type=jnp.float32
    )
    grad_w = col_part
    grad_h, grad_w = (grad_h, grad_w)
    nodes_all = lax.axis_size("blk") * blocks_here * tile_size
    weight_grad = lax.psum(grad_w, "blk") * (1.0 / math.sqrt(nodes_all))
    grad_hb = grad_h.astype(jnp.bfloat16)
    slot_count = tiles.shape[1]
    slot_ids = jnp.arange(slot_count, dtype=jnp.int32)
    live = (slot_ids[None, :] < live_count[:, None]).astype(jnp.float32).reshape(-1)
    contrib = jnp.einsum("bkij,bfi->bkfj", tiles, grad_hb, preferred_element_type=jnp.float32)
    flat_terms = contrib.reshape(blocks_here * slot_count, cols_here * tile_size)
    targets = col_block.reshape(-1)
    slabs = lax.axis_size("blk")
    own_slab = lax.axis_index("blk")
    target_slab = targets // blocks_here
    window_slot = (target_slab - own_slab + REACH + slabs) % slabs
    position = window_slot * blocks_here + targets % blocks_here
    window_rows = (2 * REACH + 1) * blocks_here
    row_ids = jnp.arange(window_rows, dtype=jnp.int32)
    selector = (position[None, :] == row_ids[:, None]).astype(jnp.float32) * live[None, :]
    window = jnp.dot(
        selector, flat_terms, preferred_element_type=jnp.float32, precision=lax.Precision.HIGHEST
    )
    window = window.reshape(2 * REACH + 1, blocks_here, cols_here, tile_size)
    input_grad = window[REACH]
    upward = window[2 * REACH]
    downward = window[0]
    for step in range(REACH):
        upward = from_behind(upward, "blk", 1)
        downward = from_behind(downward, "blk", -1)
        if step + 1 < REACH:
            upward = upward + window[2 * REACH - step - 1]
            downward = downward + window[step + 1]
    input_grad = input_grad + upward + downward
    return (input_grad.astype(jnp.bfloat16), weight_grad)


def solution(mesh):
    placed = (
        P("blk", "rep", None),
        P("blk", "rep", None),
        P("blk", "rep", None),
        P("rep", None),
        P("blk", None, None, None),
        P("blk", None),
        P("blk"),
    )
    return jax.shard_map(
        on_device,
        mesh=mesh,
        in_specs=placed,
        out_specs=(P("blk", "rep", None), P("rep", None)),
        check_vma=False,
    )
```

profile of v0, /device:TPU:0, one launch (start us, length us, event | category | flops | bytes accessed | tf_op | source)
XLA Modules:
  0.0 174.0 jit_solution(14960853211397327882)
XLA Ops:
  7.2 1.9 %convert_multiply_fusion = bf16[32,32,128]{2,1,0:T(8,128)(2,1)} fusion(bf16[32,32,128]{2,1,0:T(8,128)(2,1)} %param.7, s32[32,32,128]{2,1,0:T(8,128)} %param.8), kind=kLoop, calls=%fused_computation.19 | loop fusion | flops 262144 | bytes 1048576 | tf_op jit(solution)/shard_map/mul | solution.py:20
  9.1 0.8 copy.9
  9.9 0.1 reshape.102
  10.0 0.7 fusion.13
  10.7 0.1 reshape.104
  10.8 43.8 %all-gather.2.cloned.1.call-done = bf16[32,256,128]{2,1,0:T(8,128)(2,1)} async-done(((bf16[32,32,128]{2,1,0:T(8,128)(2,1)}), bf16[32,256,128]{2,1,0:T(8,128)(2,1)}) %all-gather.2.cloned.1.call-update) | async-done | bytes 2097168 | tf_op jit(solution)/shard_map/all_gather | solution.py:21
  54.6 9.9 %fusion.4 = f32[32,32,16,128]{3,1,2,0:T(8,128)} fusion(bf16[32,16,128,128]{3,2,1,0:T(8,128)(2,1)} %param.11, bf16[32,256,128]{2,1,0:T(8,128)(2,1)} %all-gather.2.cloned.1.call-done, bf16[32,256]{1,0:T(8,128)(2,1)} %param.10), kind=kOutput, calls=%fused_computation.6 | convolution fusion | flops 604110848 | bytes 27279360 | tf_op jit(solution)/shard_map/bkij,bfi->bkfj/dot_general | solution.py:34
  64.5 11.3 %fusion = f32[160,4096]{1,0:T(8,128)S(1)} fusion(f32[64,8,32,128]{3,2,1,0:T(8,128)} %bitcast.46, f32[512]{0:T(512)S(1)} %reshape.104, s32[512]{0:T(512)S(1)} %fusion.18), kind=kOutput, calls=%fused_computation | convolution fusion | flops 4026695680 | bytes 11014144 | tf_op jit(solution)/shard_map/dot_general | solution.py:45
  75.9 0.2 slice_bitcast_fusion.4
  76.0 0.1 copy.13
  76.1 0.1 collective-permute-start
  76.2 0.1 copy.15
  76.3 5.4 %collective-permute-start.2 = (f32[32,32,128]{2,1,0:T(8,128)S(1)}, f32[32,32,128]{2,1,0:T(8,128)S(1)}, u32[]{:S(2)}, u32[]{:S(2)}) collective-permute-start(f32[32,32,128]{2,1,0:T(8,128)S(1)} %bitcast.47), channel_id=1, source_target_pairs={{0,120},{8,0},{16,8},{24,16},{32,24},{40,32},{48,40},{56,48},{64,5... | collective-permute-start | bytes 1572872 | tf_op jit(solution)/shard_map/ppermute | solution.py:13
  81.7 0.1 copy.16
  81.8 0.1 copy.14
  81.9 8.8 %collective-permute-done = f32[32,32,128]{2,1,0:T(8,128)S(1)} collective-permute-done((f32[32,32,128]{2,1,0:T(8,128)S(1)}, f32[32,32,128]{2,1,0:T(8,128)S(1)}, u32[]{:S(2)}, u32[]{:S(2)}) %collective-permute-start) | collective-permute-done | bytes 524320 | tf_op jit(solution)/shard_map/ppermute | solution.py:13
  90.8 0.1 bitcast_add_fusion.1
  91.0 0.1 bitcast_add_fusion
  91.0 5.4 %collective-permute-start.3 = (f32[32,32,128]{2,1,0:T(8,128)S(1)}, f32[32,32,128]{2,1,0:T(8,128)S(1)}, u32[]{:S(2)}, u32[]{:S(2)}) collective-permute-start(f32[32,32,128]{2,1,0:T(8,128)S(1)} %bitcast_add_fusion), channel_id=1, source_target_pairs={{0,120},{8,0},{16,8},{24,16},{32,24},{40,32},{48,40},{56,48},{64,5... | collective-permute-start | bytes 1572872 | tf_op jit(solution)/shard_map/ppermute | solution.py:13
  96.4 0.1 copy.12
  96.6 0.7 convolution_bitcast_fusion
  97.3 68.4 %psum.7 = f32[32,256]{1,0:T(8,128)S(1)} all-reduce(f32[32,256]{1,0:T(8,128)S(1)} %convolution_bitcast_fusion), channel_id=1, replica_groups=mesh['blk'=16,'rep'=8] {'blk'}, use_global_device_ids=true, to_apply=%region_0.0 | all-reduce | flops 8192 | bytes 65536 | tf_op jit(solution)/shard_map/psum | solution.py:29
  165.6 0.6 broadcast_multiply_fusion
  166.3 0.9 fusion.6
  (11 shorter events, 0.2 us)
Async XLA Ops:
  7.2 89.4 %copy-start = (bf16[32,32,128]{2,1,0:T(8,128)(2,1)S(1)}, bf16[32,32,128]{2,1,0:T(8,128)(2,1)}, u32[]{:S(2)}) copy-start(bf16[32,32,128]{2,1,0:T(8,128)(2,1)} %param.9) | copy-start | bytes 786436
  7.2 47.5 %all-gather.2.cloned.1.call-start = ((), (), s32[]{:S(2)}) async-start(), calls=%async_computation | async-start | bytes 2359296 | tf_op jit(solution)/shard_map/all_gather | solution.py:21
  76.1 14.6 %collective-permute-start = (f32[32,32,128]{2,1,0:T(8,128)S(1)}, f32[32,32,128]{2,1,0:T(8,128)S(1)}, u32[]{:S(2)}, u32[]{:S(2)}) collective-permute-start(f32[32,32,128]{2,1,0:T(8,128)S(1)} %bitcast.48), channel_id=1, source_target_pairs={{0,8},{8,16},{16,24},{24,32},{32,40},{40,48},{48,56},{56,64},{64,7... | collective-permute-start | bytes 1572872 | tf_op jit(solution)/shard_map/ppermute | solution.py:13
  76.3 14.6 %collective-permute-start.2 = (f32[32,32,128]{2,1,0:T(8,128)S(1)}, f32[32,32,128]{2,1,0:T(8,128)S(1)}, u32[]{:S(2)}, u32[]{:S(2)}) collective-permute-start(f32[32,32,128]{2,1,0:T(8,128)S(1)} %bitcast.47), channel_id=1, source_target_pairs={{0,120},{8,0},{16,8},{24,16},{32,24},{40,32},{48,40},{56,48},{64,5... | collective-permute-start | bytes 1572872 | tf_op jit(solution)/shard_map/ppermute | solution.py:13
  81.8 14.7 %copy-start.1 = (bf16[32,256,128]{2,1,0:T(8,128)(2,1)S(1)}, bf16[32,256,128]{2,1,0:T(8,128)(2,1)}, u32[]{:S(2)}) copy-start(bf16[32,256,128]{2,1,0:T(8,128)(2,1)} %all-gather.2.cloned.1.call-done) | copy-start | bytes 6291460
  90.9 75.4 %collective-permute-start.1 = (f32[32,32,128]{2,1,0:T(8,128)S(1)}, f32[32,32,128]{2,1,0:T(8,128)S(1)}, u32[]{:S(2)}, u32[]{:S(2)}) collective-permute-start(f32[32,32,128]{2,1,0:T(8,128)S(1)} %bitcast_add_fusion.1), channel_id=1, source_target_pairs={{0,8},{8,16},{16,24},{24,32},{32,40},{40,48},{48,56},{56,64},{64,7... | collective-permute-start | bytes 1572872 | tf_op jit(solution)/shard_map/ppermute | solution.py:13
  91.0 75.2 %collective-permute-start.3 = (f32[32,32,128]{2,1,0:T(8,128)S(1)}, f32[32,32,128]{2,1,0:T(8,128)S(1)}, u32[]{:S(2)}, u32[]{:S(2)}) collective-permute-start(f32[32,32,128]{2,1,0:T(8,128)S(1)} %bitcast_add_fusion), channel_id=1, source_target_pairs={{0,120},{8,0},{16,8},{24,16},{32,24},{40,32},{48,40},{56,48},{64,5... | collective-permute-start | bytes 1572872 | tf_op jit(solution)/shard_map/ppermute | solution.py:13
Sparse Core Ops, SparseCore 0:
  10.2 44.3 all-gather.1
where the time goes:
time: 174 us
  blocking collectives  68.4 us (39%)
  waiting for transfers between devices  52.7 us (30%)
  matrix products  21.9 us (13%)
  between operations  14.1 us (8%)
  starting transfers between devices  11 us (6%)
  other arithmetic  4.3 us (2%)
    psum x1, blocking collectives, on_device(): weight_grad = lax.psum(grad_w, 'blk') * (1.0 / math.sqrt(nodes_all))  68.4 us
    all_gather x1, waiting for transfers between devices, on_device(): gathered_part = lax.all_gather(grad_z, 'rep', axis=1, tiled=True)  43.8 us
    dot_general x1, matrix products, on_device(): jnp.dot(selector, flat_terms, preferred_element_type=jnp.float32, precisi...  11.3 us
    ppermute x4, starting transfers between devices, from_behind(): return lax.ppermute(value, axis, pairs)  11 us
    dot_general x1, matrix products, on_device(): jnp.einsum('bkij,bfi->bkfj', tiles, grad_hb, preferred_element_type=jnp.f...  9.9 us
    ppermute x4, waiting for transfers between devices, from_behind(): return lax.ppermute(value, axis, pairs)  8.83 us
  transfers between devices with their start and end apart: 5, of which 2 were waited for; matrix products, arithmetic and copies ran while one was open for 2% of the time, Pallas kernels for 0%

commit v1 on v0

--- a/solution.py
+++ b/solution.py
@@ -18,7 +18,9 @@
     cols_here = cotangent.shape[1]
     tile_size = cotangent.shape[2]
     grad_z = cotangent * relu_mask.astype(jnp.bfloat16)
-    gathered_part = lax.all_gather(grad_z, "rep", axis=1, tiled=True)
+    gathered_part = jnp.concatenate(
+        lax.all_to_all(jnp.stack([grad_z] * lax.axis_size("rep")), "rep", 0, 0), axis=1
+    )
     grad_h = jnp.einsum("io,bon->bin", weight, gathered_part, preferred_element_type=jnp.float32)
     col_part = jnp.einsum(
         "bin,bon->io", aggregated, gathered_part, preferred_element_type=jnp.float32

time: 174 us -> 155 us (0.89)
  waiting for transfers between devices: 52.7 us -> 34.2 us
  between operations: 14.1 us -> 0.75 us
  starting transfers between devices: 11 us -> 17.3 us
  local copies, waits for them, and re-layouts: 1.6 us -> 6.15 us
    all_gather x1 -> x0, waiting for transfers between devices: 43.8 us -> none  [on_device(): gathered_part = lax.all_gather(grad_z, 'rep', axis=1, tiled=True)]
    all_to_all x0 -> x1, waiting for transfers between devices: none -> 25.7 us  [on_device(): lax.all_to_all(jnp.stack([grad_z] * lax.axis_size('rep')), 'rep', 0, 0)]
    all_to_all x0 -> x1, starting transfers between devices: none -> 6.46 us  [on_device(): lax.all_to_all(jnp.stack([grad_z] * lax.axis_size('rep')), 'rep', 0, 0)]
    reshape x0 -> x1, local copies, waits for them, and re-layouts: none -> 2.21 us  [on_device(): jnp.concatenate(lax.all_to_all(jnp.stack([grad_z] * lax.axis_size('rep'))...]
where the time goes in v1:
time: 155 us; the launch traced here: 154 us
  blocking collectives  68.6 us (44%)
  waiting for transfers between devices  34.2 us (22%)
  matrix products  21.1 us (14%)
  starting transfers between devices  17.3 us (11%)
  local copies, waits for them, and re-layouts  6.15 us (4%)
  other arithmetic  5.58 us (4%)
    psum x1, blocking collectives, on_device(): weight_grad = lax.psum(grad_w, 'blk') * (1.0 / math.sqrt(nodes_all))  68.6 us
    all_to_all x1, waiting for transfers between devices, on_device(): lax.all_to_all(jnp.stack([grad_z] * lax.axis_size('rep')), 'rep', 0, 0)  25.7 us
    dot_general x1, matrix products, on_device(): jnp.dot(selector, flat_terms, preferred_element_type=jnp.float32, precisi...  11.3 us
    ppermute x4, starting transfers between devices, from_behind(): return lax.ppermute(value, axis, pairs)  10.8 us
    dot_general x1, matrix products, on_device(): jnp.einsum('bkij,bfi->bkfj', tiles, grad_hb, preferred_element_type=jnp.f...  9.16 us
    ppermute x4, waiting for transfers between devices, from_behind(): return lax.ppermute(value, axis, pairs)  8.5 us
    all_to_all x1, starting transfers between devices, on_device(): lax.all_to_all(jnp.stack([grad_z] * lax.axis_size('rep')), 'rep', 0, 0)  6.46 us
  transfers between devices with their start and end apart: 5, of which 2 were waited for; matrix products, arithmetic and copies ran while one was open for 2% of the time, Pallas kernels for 0%

profile of v1, /device:TPU:0, one launch (start us, length us, event | category | flops | bytes accessed | tf_op | source)
XLA Modules:
  0.0 153.7 jit_solution(14500199615356821010)
XLA Ops:
  0.6 1.2 convert_multiply_fusion
  1.8 1.7 %stack.2 = bf16[8,32,32,128]{3,2,1,0:T(8,128)(2,1)} broadcast(bf16[32,32,128]{2,1,0:T(8,128)(2,1)S(1)} %convert_multiply_fusion), dimensions={1,2,3} | broadcast | bytes 2359296 | tf_op jit(solution)/shard_map/stack | solution.py:22
  3.5 6.5 %all-to-all-start = ((bf16[8,32,32,128]{3,2,1,0:T(8,128)(2,1)}), bf16[8,32,32,128]{3,2,1,0:T(8,128)(2,1)S(1)}, u32[]{:S(2)}, u32[]{:S(2)}) async-start(bf16[8,32,32,128]{3,2,1,0:T(8,128)(2,1)} %stack.2), calls=%async_computation | async-start | bytes 4194304 | tf_op jit(solution)/shard_map/all_to_all | solution.py:22
  10.1 0.1 reshape.110
  10.4 25.7 %all-to-all-done = bf16[8,32,32,128]{3,2,1,0:T(8,128)(2,1)S(1)} async-done(((bf16[8,32,32,128]{3,2,1,0:T(8,128)(2,1)}), bf16[8,32,32,128]{3,2,1,0:T(8,128)(2,1)S(1)}, u32[]{:S(2)}, u32[]{:S(2)}) %all-to-all-start) | async-done | bytes 2097184 | tf_op jit(solution)/shard_map/all_to_all | solution.py:22
  36.0 1.3 copy-done.1
  37.4 2.2 %copy.11 = bf16[32,8,32,128]{3,2,1,0:T(8,128)(2,1)S(1)} copy(bf16[32,8,32,128]{3,2,0,1:T(8,128)(2,1)} %bitcast.51) | data formatting | bytes 4194304 | tf_op jit(solution)/shard_map/reshape | solution.py:21
  39.6 9.2 %fusion.4 = f32[32,32,16,128]{3,1,2,0:T(8,128)} fusion(bf16[32,16,128,128]{3,2,1,0:T(8,128)(2,1)} %param.11, bf16[32,256,128]{2,1,0:T(8,128)(2,1)S(1)} %bitcast.49, bf16[32,256]{1,0:T(8,128)(2,1)S(1)} %copy-done.2), kind=kOutput, calls=%fused_computation.6 | convolution fusion | flops 604110848 | bytes 27279360 | tf_op jit(solution)/shard_map/bkij,bfi->bkfj/dot_general | solution.py:36
  48.8 11.3 %fusion = f32[160,4096]{1,0:T(8,128)S(1)} fusion(f32[64,8,32,128]{3,2,1,0:T(8,128)} %bitcast.48, f32[512]{0:T(512)S(1)} %reshape.114, s32[512]{0:T(512)S(1)} %fusion.18), kind=kOutput, calls=%fused_computation | convolution fusion | flops 4026695680 | bytes 11014144 | tf_op jit(solution)/shard_map/dot_general | solution.py:47
  60.1 0.2 slice_bitcast_fusion.4
  60.2 0.1 copy.15
  60.4 0.1 copy.17
  60.5 5.4 %collective-permute-start.2 = (f32[32,32,128]{2,1,0:T(8,128)S(1)}, f32[32,32,128]{2,1,0:T(8,128)S(1)}, u32[]{:S(2)}, u32[]{:S(2)}) collective-permute-start(f32[32,32,128]{2,1,0:T(8,128)S(1)} %bitcast.52), channel_id=1, source_target_pairs={{0,120},{8,0},{16,8},{24,16},{32,24},{40,32},{48,40},{56,48},{64,5... | collective-permute-start | bytes 1572872 | tf_op jit(solution)/shard_map/ppermute | solution.py:13
  65.9 0.1 copy.18
  66.0 0.1 copy.16
  66.1 8.5 %collective-permute-done = f32[32,32,128]{2,1,0:T(8,128)S(1)} collective-permute-done((f32[32,32,128]{2,1,0:T(8,128)S(1)}, f32[32,32,128]{2,1,0:T(8,128)S(1)}, u32[]{:S(2)}, u32[]{:S(2)}) %collective-permute-start) | collective-permute-done | bytes 524320 | tf_op jit(solution)/shard_map/ppermute | solution.py:13
  74.6 0.9 bitcast_add_fusion.1
  75.6 0.9 bitcast_add_fusion
  76.4 5.4 %collective-permute-start.3 = (f32[32,32,128]{2,1,0:T(8,128)}, f32[32,32,128]{2,1,0:T(8,128)}, u32[]{:S(2)}, u32[]{:S(2)}) collective-permute-start(f32[32,32,128]{2,1,0:T(8,128)} %bitcast_add_fusion), channel_id=1, source_target_pairs={{0,120},{8,0},{16,8},{24,16},{32,24},{40,32},{48,40},{56,48},{64,5... | collective-permute-start | bytes 1572872 | tf_op jit(solution)/shard_map/ppermute | solution.py:13
  81.8 0.1 copy.14
  81.9 0.7 convolution_bitcast_fusion
  82.6 68.6 %psum.7 = f32[32,256]{1,0:T(8,128)S(1)} all-reduce(f32[32,256]{1,0:T(8,128)S(1)} %convolution_bitcast_fusion), channel_id=1, replica_groups=mesh['blk'=16,'rep'=8] {'blk'}, use_global_device_ids=true, to_apply=%region_0.0 | all-reduce | flops 8192 | bytes 65536 | tf_op jit(solution)/shard_map/psum | solution.py:31
  151.2 0.6 broadcast_multiply_fusion
  151.9 1.9 %fusion.6 = bf16[32,32,128]{2,1,0:T(8,128)(2,1)} fusion(f32[32,32,128]{2,1,0:T(8,128)} %collective-permute-done.3, f32[32,32,128]{2,1,0:T(8,128)S(1)} %collective-permute-done.1, f32[4,8,32,128]{3,2,1,0:T(8,128)S(1)} %copy.14), kind=kLoop, calls=%fused_computation.11 | loop fusion | flops 393216 | bytes 1835008 | tf_op jit(solution)/shard_map/convert_element_type | solution.py:61
  (18 shorter events, 0.4 us)
Async XLA Ops:
  0.6 81.3 %copy-start = (bf16[32,32,128]{2,1,0:T(8,128)(2,1)S(1)}, bf16[32,32,128]{2,1,0:T(8,128)(2,1)}, u32[]{:S(2)}) copy-start(bf16[32,32,128]{2,1,0:T(8,128)(2,1)} %param.9) | copy-start | bytes 786436
  3.5 6.5 %copy-start.3 = (s32[32,16]{0,1:T(8,128)S(1)}, s32[32,16]{0,1:T(8,128)}, u32[]{:S(2)}) copy-start(s32[32,16]{0,1:T(8,128)} %param.12) | copy-start | bytes 6148
  3.5 6.6 %copy-start.4 = (s32[32]{0:T(128)S(1)}, s32[32]{0:T(128)}, u32[]{:S(2)}) copy-start(s32[32]{0:T(128)} %param.13) | copy-start | bytes 388
  3.5 32.5 %all-to-all-start = ((bf16[8,32,32,128]{3,2,1,0:T(8,128)(2,1)}), bf16[8,32,32,128]{3,2,1,0:T(8,128)(2,1)S(1)}, u32[]{:S(2)}, u32[]{:S(2)}) async-start(bf16[8,32,32,128]{3,2,1,0:T(8,128)(2,1)} %stack.2), calls=%async_computation | async-start | bytes 4194304 | tf_op jit(solution)/shard_map/all_to_all | solution.py:22
  10.0 29.6 %copy-start.2 = (bf16[32,256]{1,0:T(8,128)(2,1)S(1)}, bf16[32,256]{1,0:T(8,128)(2,1)}, u32[]{:S(2)}) copy-start(bf16[32,256]{1,0:T(8,128)(2,1)} %param.10) | copy-start | bytes 49156
  36.0 1.3 copy-start.1
  60.3 14.3 %collective-permute-start = (f32[32,32,128]{2,1,0:T(8,128)S(1)}, f32[32,32,128]{2,1,0:T(8,128)S(1)}, u32[]{:S(2)}, u32[]{:S(2)}) collective-permute-start(f32[32,32,128]{2,1,0:T(8,128)S(1)} %bitcast.53), channel_id=1, source_target_pairs={{0,8},{8,16},{16,24},{24,32},{32,40},{40,48},{48,56},{56,64},{64,7... | collective-permute-start | bytes 1572872 | tf_op jit(solution)/shard_map/ppermute | solution.py:13
  60.5 15.0 %collective-permute-start.2 = (f32[32,32,128]{2,1,0:T(8,128)S(1)}, f32[32,32,128]{2,1,0:T(8,128)S(1)}, u32[]{:S(2)}, u32[]{:S(2)}) collective-permute-start(f32[32,32,128]{2,1,0:T(8,128)S(1)} %bitcast.52), channel_id=1, source_target_pairs={{0,120},{8,0},{16,8},{24,16},{32,24},{40,32},{48,40},{56,48},{64,5... | collective-permute-start | bytes 1572872 | tf_op jit(solution)/shard_map/ppermute | solution.py:13
  75.5 76.3 %collective-permute-start.1 = (f32[32,32,128]{2,1,0:T(8,128)}, f32[32,32,128]{2,1,0:T(8,128)S(1)}, u32[]{:S(2)}, u32[]{:S(2)}) collective-permute-start(f32[32,32,128]{2,1,0:T(8,128)} %bitcast_add_fusion.1), channel_id=1, source_target_pairs={{0,8},{8,16},{16,24},{24,32},{32,40},{40,48},{48,56},{56,64},{64,7... | collective-permute-start | bytes 1572872 | tf_op jit(solution)/shard_map/ppermute | solution.py:13
  76.4 75.4 %collective-permute-start.3 = (f32[32,32,128]{2,1,0:T(8,128)}, f32[32,32,128]{2,1,0:T(8,128)}, u32[]{:S(2)}, u32[]{:S(2)}) collective-permute-start(f32[32,32,128]{2,1,0:T(8,128)} %bitcast_add_fusion), channel_id=1, source_target_pairs={{0,120},{8,0},{16,8},{24,16},{32,24},{40,32},{48,40},{56,48},{64,5... | collective-permute-start | bytes 1572872 | tf_op jit(solution)/shard_map/ppermute | solution.py:13
